TPU v7x, 32 devices: a whole 2x2x4 slice. The times are simulated.
32 devices in a mesh: shard: 8 (over z, x), tensor: 4 (over y, core).
Axes of the slice: x: 2, y: 2, z: 4, core: 2. Of those that a mesh axis runs over, the one named last changes fastest.
Arguments:
- att_grads: float32 [2, 4, 768, 768], P(None, None, 'shard', 'tensor'), may hold values from -6 to 6
- glu_grads: float32 [2, 4, 768, 1024], P(None, None, 'shard', 'tensor'), may hold values from -6 to 6
- att_weight: float32 [4, 768, 768], P(None, 'shard', 'tensor'), may hold values from -0.21875 to 0.21875
- att_moment: float32 [4, 768, 768], P(None, 'shard', 'tensor'), may hold values from -4 to 4
- att_second: float32 [4, 768, 768], P(None, 'shard', 'tensor'), may hold values from 0.05 to 1
- glu_weight: float32 [4, 768, 1024], P(None, 'shard', 'tensor'), may hold values from -0.21875 to 0.21875
- glu_moment: float32 [4, 768, 1024], P(None, 'shard', 'tensor'), may hold values from -4 to 4
- glu_second: float32 [4, 768, 1024], P(None, 'shard', 'tensor'), may hold values from 0.05 to 1
- att_stats: float32 [8, 2, 768, 768], P('shard', None, 'tensor'), may hold values from -1 to 10
- att_left_root: bfloat16 [8, 768, 768], P('shard', 'tensor'), may hold values from -1 to 2
- att_right_root: bfloat16 [8, 768, 768], P('shard', None, 'tensor'), may hold values from -1 to 2
- glu_left_stat: float32 [8, 768, 768], P('shard', 'tensor'), may hold values from -1 to 10
- glu_right_stat: float32 [8, 1024, 1024], P('shard', 'tensor'), may hold values from -1 to 10
- glu_left_root: bfloat16 [8, 768, 768], P('shard', 'tensor'), may hold values from -1 to 2
- glu_right_root: bfloat16 [8, 1024, 1024], P('shard', None, 'tensor'), may hold values from -1 to 2
- att_owner: int32 [4], replicated, may hold values from 0 to 7, as said below
- glu_owner: int32 [4], replicated, may hold values from 0 to 7, as said below
Outputs:
- att_weight_out: float32 [4, 768, 768], P(None, 'shard', 'tensor')
- att_moment_out: float32 [4, 768, 768], P(None, 'shard', 'tensor')
- att_second_out: float32 [4, 768, 768], P(None, 'shard', 'tensor')
- glu_weight_out: float32 [4, 768, 1024], P(None, 'shard', 'tensor')
- glu_moment_out: float32 [4, 768, 1024], P(None, 'shard', 'tensor')
- glu_second_out: float32 [4, 768, 1024], P(None, 'shard', 'tensor')
- att_stats_out: float32 [8, 2, 768, 768], P('shard', None, 'tensor')
- glu_left_out: float32 [8, 768, 768], P('shard', 'tensor')
- glu_right_out: float32 [8, 1024, 1024], P('shard', 'tensor')
Inputs may be any that keep to these rules, and one draw needn't show every extreme that they name: `att_owner`: distinct owners; no owner holds more than one attention matrix. `glu_owner`: distinct owners; no owner holds more than one GeGLU block; in every draw some owner holds an attention matrix and a GeGLU block.
All inputs are finite; a program needn't handle non-finite values.
Results may differ from a plain program's by a relative error of at most 0.0014.
Values may be sent and summed in bfloat16 or wider, within the bound.
No kernel may reach another device: no remote copies, remote signals or barrier semaphores. Data moves between devices by JAX's collectives and lax.ppermute only.
A program may use at most 128 MiB of HBM per device.

v0:
```python
import functools

import jax
import jax.numpy as jnp
from jax import lax
from jax.experimental import pallas as pl
from jax.experimental.pallas import tpu as pltpu
from jax.sharding import PartitionSpec as P

beta_one = 0.9
beta_two = 0.999
beta_stat = 0.999
adam_eps = 1e-08
graft_eps = 1e-06
learn_rate = 0.01

bf16 = jnp.bfloat16
f32 = jnp.float32
LANES = 128
VMEM = pl.BlockSpec(memory_space=pltpu.VMEM)
BRIEF = pl.CostEstimate(flops=1_000_000_000, bytes_accessed=1024, transcendentals=0)
LIMIT = pltpu.CompilerParams(vmem_limit_bytes=16 << 20)
SMEM = pl.BlockSpec(memory_space=pltpu.SMEM)
HBM = pl.BlockSpec(memory_space=pltpu.HBM)


def in_hbm(value):
    return pltpu.with_memory_space_constraint(value, pltpu.HBM)


def round_up(value, step):
    return -(-value // step) * step


def folds(rows, cols):
    return cols == LANES + LANES // 2 and rows % 32 == 0


def packed_shape(rows, cols, totals):
    lanes = round_up(cols, LANES)
    if folds(rows, cols):
        return (rows + rows // 2 + round_up(3 * totals, 8), LANES)
    return (rows, lanes) if lanes > cols else (round_up(rows + 3 * totals, 8), cols)


def pieces(totals, shape):
    row = lax.broadcasted_iota(jnp.int32, shape, 0)
    column = lax.broadcasted_iota(jnp.int32, shape, 1)
    value = jnp.zeros(shape, f32)
    for n, total in enumerate(totals):
        rest = jnp.broadcast_to(total, shape)
        for m in range(3):
            piece = rest.astype(bf16).astype(f32)
            value = jnp.where(row == 3 * n + m, piece, value)
            rest = rest - piece
    return jnp.where(column == 0, value, 0.0).astype(bf16)


def pack(ref, value, totals):
    rows, cols = value.shape
    high, wide = ref.shape
    if folds(rows, cols):
        half, side = rows // 2, value[:, LANES:]
        ref[:rows, :] = value[:, :LANES].astype(bf16)
        ref[rows : rows + half, :] = jnp.concatenate([side[:half], side[half:]], axis=1).astype(bf16)
        if totals:
            ref[rows + half :, :] = pieces(totals, (high - rows - half, wide))
    elif wide > cols:
        ref[:, :cols] = value.astype(bf16)
        ref[:, cols:] = pieces(totals, (high, wide - cols))
    else:
        ref[:rows, :] = value.astype(bf16)
        if totals:
            ref[rows:, :] = pieces(totals, (high - rows, wide))


def unpack(ref, rows, cols, start=0, count=None):
    count = ref.shape[0] if count is None else count
    span = pl.ds(start, count)
    if not folds(rows, cols):
        return ref[span, :rows, :cols].reshape(count * rows, cols)
    side = ref[span, rows : rows + rows // 2, :]
    side = jnp.concatenate([side[:, :, : LANES // 2], side[:, :, LANES // 2 :]], axis=1)
    return jnp.concatenate([ref[span, :rows, :], side], axis=2).reshape(count * rows, cols)


def unpack_total(ref, rows, cols, n, start=0, count=None):
    count = ref.shape[0] if count is None else count
    span = pl.ds(start, count)
    if folds(rows, cols):
        extra = ref[span, rows + rows // 2 :, :]
    elif ref.shape[2] > cols:
        extra = ref[span, :, cols:]
    else:
        extra = ref[span, rows:, :]
    row = lax.broadcasted_iota(jnp.int32, extra.shape, 1)
    mine = jnp.where((row >= 3 * n) & (row < 3 * n + 3), extra.astype(f32), 0.0)
    return jnp.sum(jnp.sum(mine, axis=0), axis=(0, 1), keepdims=True)


def adam_kernel(owner, grads, moment, second, packed, moment_out, second_out):
    packed[...] = jnp.zeros_like(packed)

    def unit(u, carry):
        summed = grads[0, u]
        for micro in range(1, grads.shape[0]):
            summed = summed + grads[micro, u]
        moment_new = beta_one * moment[u] + (1.0 - beta_one) * summed
        second_new = beta_two * second[u] + (1.0 - beta_two) * summed * summed
        direction = moment_new / (jnp.sqrt(second_new) + adam_eps)
        moment_out[u] = moment_new
        second_out[u] = second_new
        total = jnp.sum(direction * direction, axis=(0, 1), keepdims=True)
        pack(packed.at[owner[u]], summed, (total,))
        return carry

    lax.fori_loop(0, moment.shape[0], unit, 0, unroll=moment.shape[0] <= 4)


def adam_part(owner, grads, moment, second, owners, params):
    rows, cols = moment.shape[1:]
    return pl.pallas_call(
        adam_kernel,
        out_shape=(
            jax.ShapeDtypeStruct((owners, *packed_shape(rows, cols, 1)), bf16),
            jax.ShapeDtypeStruct(moment.shape, f32),
            jax.ShapeDtypeStruct(second.shape, f32),
        ),
        in_specs=[SMEM, VMEM, VMEM, VMEM],
        out_specs=(VMEM, VMEM, VMEM),
        compiler_params=params,
        cost_estimate=pl.CostEstimate(
            flops=10_000_000_000, bytes_accessed=32 * moment.size, transcendentals=moment.size
        ),
    )(owner, grads, moment, second)


def holds(owner):
    me = lax.axis_index("shard")
    found = owner[0] == me
    for unit in range(1, owner.shape[0]):
        found = jnp.logical_or(found, owner[unit] == me)
    return found


def shampoo_kernel(rows, cols, turned, embed, owner, *refs):
    tensor = lax.axis_size("tensor")
    left, grad = refs[:tensor], refs[tensor : 2 * tensor]
    root_hbm, *outs, whole, blocks, done, root, arrived = refs[2 * tensor :]
    part = lax.axis_index("tensor")

    @pl.when(holds(owner))
    def _():
        depth = left[0].shape[0]
        fetch = pltpu.make_async_copy(root_hbm, root, arrived)
        fetch.start()
        adam_sq = jnp.zeros((1, 1), f32)
        for k in range(tensor):
            band = pl.ds(pl.multiple_of((part ^ k) * depth, depth), depth)
            whole[band, :] = left[k][...]
            blocks[part ^ k] = unpack(grad[k], rows, cols)
            adam_sq = adam_sq + unpack_total(grad[k], rows, cols, 0)
        half = jnp.zeros((whole.shape[0], cols), f32)
        fetch.wait()
        for k in range(tensor):
            span = slice(k * cols, (k + 1) * cols)
            if turned:
                sides, right = (((1,), (1,)), ((), ())), root[0, :, span]
            else:
                sides, right = (((1,), (0,)), ((), ())), root[0, span, :]
            half = half + lax.dot_general(blocks[k], right, sides, preferred_element_type=f32)
        total = jnp.dot(whole[...], half.astype(bf16), preferred_element_type=f32)
        norm = jnp.sum(total * total, axis=(0, 1), keepdims=True)
        if embed:
            done[...] = total
            for slot in range(outs[0].shape[0]):
                value = done[slot * rows : (slot + 1) * rows, :]
                pack(outs[0].at[slot], value, (norm, adam_sq))
        else:
            for ref, value in zip(outs, (total, norm, adam_sq)):
                ref[...] = jnp.broadcast_to(value, ref.shape)

    @pl.when(jnp.logical_not(holds(owner)))
    def _():
        for ref in outs:
            ref[...] = jnp.zeros_like(ref)


def shampoo_part(owner, left, grad, root, rows, embed):
    cols = root.shape[2]
    depth = left[0].shape[1]
    tensor = len(left)
    turned = cols % LANES != 0
    if turned:
        root = jnp.swapaxes(root, 1, 2)
    if embed:
        shapes = (jax.ShapeDtypeStruct((depth // rows, *packed_shape(rows, cols, 2)), bf16),)
    else:
        small = jax.ShapeDtypeStruct((8, LANES), f32)
        shapes = (jax.ShapeDtypeStruct((depth, cols), f32), small, small)
    return pl.pallas_call(
        functools.partial(shampoo_kernel, rows, cols, turned, embed),
        out_shape=shapes,
        in_specs=[SMEM] + [VMEM] * (2 * tensor) + [HBM],
        out_specs=(VMEM,) * len(shapes),
        scratch_shapes=[
            pltpu.VMEM((depth, depth), bf16),
            pltpu.VMEM((tensor, depth, cols), bf16),
            pltpu.VMEM((depth, cols) if embed else (8, LANES), f32),
            pltpu.VMEM(root.shape, bf16),
            pltpu.SemaphoreType.DMA(()),
        ],
        compiler_params=LIMIT,
        cost_estimate=BRIEF,
    )(owner, *left, *grad, in_hbm(root))


def stats_kernel(rows, cols, paired, owner, *refs):
    tensor = lax.axis_size("tensor")
    grad, count = refs[:tensor], 1 if paired else 2
    stats, outs = refs[tensor : tensor + count], refs[tensor + count : tensor + 2 * count]
    square, held, (arrived, sent) = refs[tensor + 2 * count], refs[-count - 2 : -2], refs[-2:]

    def sides(group):
        return [group[0].at[0, 0], group[0].at[0, 1]] if paired else [ref.at[0] for ref in group]

    left, right = sides(held)
    fetches, stores = [], []
    for i, (source, slot, target) in enumerate(zip(sides(stats), (left, right), sides(outs))):
        fetches.append(pltpu.make_async_copy(source, slot, arrived.at[i]))
        stores.append(pltpu.make_async_copy(slot, target, sent.at[i]))
        fetches[-1].start()
    part = lax.axis_index("tensor")

    @pl.when(holds(owner))
    def _():
        high = left.shape[0]
        total = jnp.zeros(left.shape, f32)
        mine = unpack(grad[0], rows, cols)
        for k in range(tensor):
            columns = unpack(grad[k], rows, cols)
            slots = high // rows
            band = unpack(grad[k], rows, cols, part * slots, slots)
            total = total + lax.dot_general(
                band, columns, (((1,), (1,)), ((), ())), preferred_element_type=f32
            )
            square[part ^ k] = lax.dot_general(
                mine, columns, (((0,), (0,)), ((), ())), preferred_element_type=f32
            )
        fetches[0].wait()
        left[...] = beta_stat * left[...] + (1.0 - beta_stat) * total
        stores[0].start()
        fetches[1].wait()
        for k in range(tensor):
            span = slice(k * cols, (k + 1) * cols)
            right[:, span] = beta_stat * right[:, span] + (1.0 - beta_stat) * square[k]
        stores[1].start()
        for store in stores:
            store.wait()

    @pl.when(jnp.logical_not(holds(owner)))
    def _():
        for fetch, store in zip(fetches, stores):
            fetch.wait()
            store.start()
        for store in stores:
            store.wait()


def stats_part(owner, grad, stats, rows, cols):
    tensor = len(grad)
    depth = tensor * cols
    return pl.pallas_call(
        functools.partial(stats_kernel, rows, cols, len(stats) == 1),
        out_shape=tuple(jax.ShapeDtypeStruct(value.shape, f32) for value in stats),
        in_specs=[SMEM] + [VMEM] * tensor + [HBM] * len(stats),
        out_specs=(HBM,) * len(stats),
        scratch_shapes=[pltpu.VMEM((tensor, cols, cols), f32)]
        + [pltpu.VMEM(value.shape, f32) for value in stats]
        + [pltpu.SemaphoreType.DMA((2,)), pltpu.SemaphoreType.DMA((2,))],
        compiler_params=LIMIT,
        cost_estimate=pl.CostEstimate(
            flops=4 * depth * depth * cols,
            bytes_accessed=8 * sum(value.size for value in stats) + 2 * depth * depth,
            transcendentals=0,
        ),
    )(owner, *grad, *[in_hbm(value) for value in stats])


def weight_kernel(owner, weight, back, *refs):
    *norm, out = refs
    rows, cols = weight.shape[1:]

    def unit(u, carry):
        update = unpack(back, rows, cols, owner[u], 1).astype(f32)
        if norm:
            adam, *norms = norm
            total = norms[0][u]
            for other in norms[1:]:
                total = total + other[u]
            update = jnp.sqrt(adam[u] / (total + graft_eps))[:1, :1] * update
        out[u] = weight[u] - learn_rate * update
        return carry

    lax.fori_loop(0, weight.shape[0], unit, 0, unroll=weight.shape[0] <= 4)


def weight_part(owner, weight, back, *norm):
    return pl.pallas_call(
        weight_kernel,
        out_shape=jax.ShapeDtypeStruct(weight.shape, f32),
        in_specs=[SMEM] + [VMEM] * (2 + len(norm)),
        out_specs=VMEM,
        compiler_params=LIMIT,
        cost_estimate=pl.CostEstimate(
            flops=2 * weight.size, bytes_accessed=12 * weight.size, transcendentals=0
        ),
    )(owner, weight, back, *norm)


def totals_kernel(rows, cols, owner, back, norm, adam):
    def unit(u, carry):
        for n, ref in enumerate((norm, adam)):
            total = unpack_total(back, rows, cols, n, owner[u], 1)
            ref[u] = jnp.broadcast_to(total, ref.shape[1:])
        return carry

    lax.fori_loop(0, norm.shape[0], unit, 0, unroll=norm.shape[0] <= 4)


def totals_part(owner, back, rows, cols):
    small = jax.ShapeDtypeStruct((owner.shape[0], 8, LANES), f32)
    norm, adam = pl.pallas_call(
        functools.partial(totals_kernel, rows, cols),
        out_shape=(small, small),
        in_specs=[SMEM, VMEM],
        out_specs=(VMEM, VMEM),
        compiler_params=LIMIT,
        cost_estimate=BRIEF,
    )(owner, back)
    return adam, *all_norms(norm)


def all_norms(norm):
    return [norm] + [flip(norm, k) for k in range(1, lax.axis_size("tensor"))]


def flip(value, bits):
    size = lax.axis_size("tensor")
    return lax.ppermute(value, "tensor", [(i, i ^ bits) for i in range(size)])


def spread_first(value):
    return value, flip(value, lax.axis_size("tensor") // 2)


def spread_rest(value, far):
    bit = lax.axis_size("tensor") // 2
    held = {0: value, bit: far}
    bit //= 2
    while bit:
        for k in sorted(held):
            held[k | bit] = flip(held[k], bit)
        bit //= 2
    return [held[k] for k in range(len(held))]


def after(value, *others):
    return lax.optimization_barrier((value, *others))[0]


def over_shard(value):
    return lax.all_to_all(value, "shard", split_axis=0, concat_axis=0, tiled=True)


def scale_kernel(done, adam, *refs):
    norm, out = refs[:-1], refs[-1]
    total = norm[0][...]
    for other in norm[1:]:
        total = total + other[...]
    scale = jnp.sqrt(adam[...] / (total + graft_eps))[:1, :1]
    rows = done.shape[0] // out.shape[0]
    for slot in range(out.shape[0]):
        pack(out.at[slot], scale * done[slot * rows : (slot + 1) * rows, :], ())


def grafted(done, norm, adam, owners):
    depth, cols = done.shape
    norms = all_norms(norm)
    return pl.pallas_call(
        scale_kernel,
        out_shape=jax.ShapeDtypeStruct((owners, *packed_shape(depth // owners, cols, 0)), bf16),
        in_specs=[VMEM] * (2 + len(norms)),
        out_specs=VMEM,
        compiler_params=LIMIT,
        cost_estimate=pl.CostEstimate(
            flops=done.size, bytes_accessed=6 * done.size, transcendentals=0
        ),
    )(done, adam, *norms)


def per_device(
    att_grads,
    glu_grads,
    att_weight,
    att_moment,
    att_second,
    glu_weight,
    glu_moment,
    glu_second,
    att_stats,
    att_left_root,
    att_right_root,
    glu_left_stat,
    glu_right_stat,
    glu_left_root,
    glu_right_root,
    att_owner,
    glu_owner,
):
    owners = lax.axis_size("shard")
    rows = att_weight.shape[1]
    glu_packed, glu_moment_out, glu_second_out = adam_part(
        glu_owner, glu_grads, glu_moment, glu_second, owners, None
    )
    glu_root, glu_root_far = spread_first(glu_left_root[0])
    att_root, att_root_far = spread_first(att_left_root[0])
    att_packed, att_moment_out, att_second_out = adam_part(
        att_owner,
        after(att_grads, glu_root_far, att_root_far),
        att_moment,
        att_second,
        owners,
        LIMIT,
    )
    glu_near, glu_far = spread_first(after(over_shard(glu_packed), att_packed))
    glu_beside = flip(glu_near, 1)
    glu_root, glu_root_far, _ = lax.optimization_barrier((glu_root, glu_root_far, glu_beside))
    glu_left = spread_rest(glu_root, glu_root_far)
    glu_grad = spread_rest(glu_near, glu_far)
    (glu_done,) = shampoo_part(glu_owner, glu_left, glu_grad, glu_right_root, rows, True)
    att_near, att_far = spread_first(after(over_shard(att_packed), glu_done))
    att_left = spread_rest(*lax.optimization_barrier((att_root, att_root_far, att_near))[:2])
    att_grad = spread_rest(att_near, att_far)
    glu_back = over_shard(after(glu_done, att_grad[1]))
    att_done = shampoo_part(att_owner, att_left, att_grad, att_right_root, rows, False)
    glu_left_out, glu_right_out = stats_part(
        glu_owner,
        [after(glu_grad[0], att_done[0]), *glu_grad[1:]],
        (glu_left_stat, glu_right_stat),
        rows,
        glu_weight.shape[2],
    )
    att_done = (after(att_done[0], glu_left_out), *att_done[1:])
    (att_stats_out,) = stats_part(att_owner, att_grad, (att_stats,), rows, att_weight.shape[2])
    att_back = over_shard(grafted(*att_done, owners))
    glu_totals = totals_part(glu_owner, glu_back, rows, glu_weight.shape[2])
    glu_weight_out = weight_part(glu_owner, glu_weight, glu_back, *glu_totals)
    att_weight_out = weight_part(att_owner, att_weight, att_back)
    return (
        att_weight_out,
        att_moment_out,
        att_second_out,
        glu_weight_out,
        glu_moment_out,
        glu_second_out,
        att_stats_out,
        glu_left_out,
        glu_right_out,
    )


def solution(mesh):
    placed = (
        P(None, None, "shard", "tensor"),
        P(None, None, "shard", "tensor"),
        P(None, "shard", "tensor"),
        P(None, "shard", "tensor"),
        P(None, "shard", "tensor"),
        P(None, "shard", "tensor"),
        P(None, "shard", "tensor"),
        P(None, "shard", "tensor"),
        P("shard", None, "tensor", None),
        P("shard", "tensor", None),
        P("shard", None, "tensor"),
        P("shard", "tensor", None),
        P("shard", "tensor", None),
        P("shard", "tensor", None),
        P("shard", None, "tensor"),
        P(),
        P(),
    )
    return jax.shard_map(
        per_device,
        mesh=mesh,
        in_specs=placed,
        out_specs=(
            P(None, "shard", "tensor"),
            P(None, "shard", "tensor"),
            P(None, "shard", "tensor"),
            P(None, "shard", "tensor"),
            P(None, "shard", "tensor"),
            P(None, "shard", "tensor"),
            P("shard", None, "tensor", None),
            P("shard", "tensor", None),
            P("shard", "tensor", None),
        ),
        check_vma=False,
    )
```

profile of v0, /device:TPU:0, one launch (start us, length us, event | category | flops | bytes accessed | tf_op | source)
XLA Modules:
  0.0 80.8 jit_solution(1614082304182357313)
XLA Ops:
  0.6 3.0 %collective-permute-start = (bf16[192,768]{1,0:T(8,128)(2,1)}, bf16[192,768]{1,0:T(8,128)(2,1)}, u32[]{:S(2)}, u32[]{:S(2)}) collective-permute-start(bf16[192,768]{1,0:T(8,128)(2,1)} %bitcast.6), channel_id=1, source_target_pairs={{0,2},{1,3},{2,0},{3,1},{4,6},{5,7},{6,4},{7,5},{8,10},{9,11},{10,... | collective-permute-start | bytes 884744 | tf_op jit(solution)/shard_map/ppermute | solution.py:350
  3.8 2.7 %shard_map.233 = (bf16[8,104,256]{2,1,0:T(8,128)(2,1)}, f32[4,96,256]{2,1,0:T(8,128)}, f32[4,96,256]{2,1,0:T(8,128)}) custom-call(s32[4]{0:T(128)} %owner.16, f32[2,4,96,256]{3,2,1,0:T(8,128)} %grads.2, f32[4,96,256]{2,1,0:T(8,128)} %moment.3, f32[4,96,256]{2,1,0:T(8,128)} %second.3), custom_call_target="tpu_custom_call" | custom-call | flops 10000000000 | bytes 3145728 | tf_op jit(solution)/shard_map/pallas_call | solution.py:122
  6.5 6.2 %all-to-all-start.1 = ((bf16[8,104,256]{2,1,0:T(8,128)(2,1)}), bf16[8,104,256]{2,1,0:T(8,128)(2,1)S(1)}, u32[]{:S(2)}, u32[]{:S(2)}) async-start(bf16[8,104,256]{2,1,0:T(8,128)(2,1)} %get-tuple-element.34), calls=%async_computation.1 | async-start | bytes 851968 | tf_op jit(solution)/shard_map/all_to_all | solution.py:373
  12.7 4.5 %collective-permute-done.1.refs_2_ = bf16[192,768]{1,0:T(8,128)(2,1)S(1)} collective-permute-done((bf16[192,768]{1,0:T(8,128)(2,1)}, bf16[192,768]{1,0:T(8,128)(2,1)S(1)}, u32[]{:S(2)}, u32[]{:S(2)}) %collective-permute-start.1) | collective-permute-done | bytes 294944 | tf_op jit(solution)/shard_map/ppermute | solution.py:350
  17.2 1.8 %shard_map.232 = (bf16[8,152,128]{2,1,0:T(8,128)(2,1)}, f32[4,96,192]{2,1,0:T(8,128)}, f32[4,96,192]{2,1,0:T(8,128)}) custom-call(s32[4]{0:T(128)S(1)} %copy-done.4, f32[2,4,96,192]{3,2,1,0:T(8,128)S(1)} %copy-done.5, f32[4,96,192]{2,1,0:T(8,128)S(1)} %copy-done.6, f32[4,96,192]{2,1,0:T(8,128)S(1)} %copy-done.7), custom_call_target="tpu_custom_call" | custom-call | flops 10000000000 | bytes 2359296 | tf_op jit(solution)/shard_map/pallas_call | solution.py:122
  19.0 5.7 %all-to-all-done.1.refs_4_.refs_0_ = bf16[8,104,256]{2,1,0:T(8,128)(2,1)S(1)} async-done(((bf16[8,104,256]{2,1,0:T(8,128)(2,1)}), bf16[8,104,256]{2,1,0:T(8,128)(2,1)S(1)}, u32[]{:S(2)}, u32[]{:S(2)}) %all-to-all-start.1) | async-done | bytes 426016 | tf_op jit(solution)/shard_map/all_to_all | solution.py:373
  24.7 1.4 %collective-permute-start.5 = (bf16[8,104,256]{2,1,0:T(8,128)(2,1)S(1)}, bf16[8,104,256]{2,1,0:T(8,128)(2,1)S(1)}, u32[]{:S(2)}, u32[]{:S(2)}) collective-permute-start(bf16[8,104,256]{2,1,0:T(8,128)(2,1)S(1)} %all-to-all-done.1.refs_4_.refs_0_), channel_id=1, source_target_pairs={{0,2},{1,3},{2,0},{3,1},{4,6},{5,7},{6,4},{7,5},{8,10},{9,11},{10,... | collective-permute-start | bytes 1277960 | tf_op jit(solution)/shard_map/ppermute | solution.py:350
  26.1 3.6 %all-to-all-start = ((bf16[8,152,128]{2,1,0:T(8,128)(2,1)}), bf16[8,152,128]{2,1,0:T(8,128)(2,1)S(1)}, u32[]{:S(2)}, u32[]{:S(2)}) async-start(bf16[8,152,128]{2,1,0:T(8,128)(2,1)} %get-tuple-element.33), calls=%async_computation | async-start | bytes 622592 | tf_op jit(solution)/shard_map/all_to_all | solution.py:373
  29.7 3.3 %collective-permute-done.5.refs_6_.refs_2_ = bf16[8,104,256]{2,1,0:T(8,128)(2,1)S(1)} collective-permute-done((bf16[8,104,256]{2,1,0:T(8,128)(2,1)S(1)}, bf16[8,104,256]{2,1,0:T(8,128)(2,1)S(1)}, u32[]{:S(2)}, u32[]{:S(2)}) %collective-permute-start.5) | collective-permute-done | bytes 426016 | tf_op jit(solution)/shard_map/ppermute | solution.py:350
  33.6 1.6 %collective-permute-done.3.refs_1_ = bf16[192,768]{1,0:T(8,128)(2,1)S(1)} collective-permute-done((bf16[192,768]{1,0:T(8,128)(2,1)S(1)}, bf16[192,768]{1,0:T(8,128)(2,1)S(1)}, u32[]{:S(2)}, u32[]{:S(2)}) %collective-permute-start.3) | collective-permute-done | bytes 294944 | tf_op jit(solution)/shard_map/ppermute | solution.py:350
  35.6 4.0 %shard_map.234 = bf16[8,104,256]{2,1,0:T(8,128)(2,1)} custom-call(s32[4]{0:T(128)S(1)} %copy-done.3, bf16[192,768]{1,0:T(8,128)(2,1)S(1)} %bitcast.5, bf16[192,768]{1,0:T(8,128)(2,1)S(1)} %collective-permute-done.3.refs_1_, bf16[192,768]{1,0:T(8,128)(2,1)S(1)} %collective-permute-done.1.refs_2_, bf16[192,768]{1,0:T(8,128)(2,1)S(1)} %collective-permute-done.4.refs_3_, ...), custom_call_target="tpu_custom_call" | custom-call | flops 1000000000 | bytes 1024 | tf_op jit(solution)/shard_map/pallas_call | solution.py:201
  40.3 1.1 %collective-permute-start.10 = (bf16[8,152,128]{2,1,0:T(8,128)(2,1)S(1)}, bf16[8,152,128]{2,1,0:T(8,128)(2,1)S(1)}, u32[]{:S(2)}, u32[]{:S(2)}) collective-permute-start(bf16[8,152,128]{2,1,0:T(8,128)(2,1)S(1)} %all-to-all-done.refs_4_.refs_0_), channel_id=1, source_target_pairs={{0,2},{1,3},{2,0},{3,1},{4,6},{5,7},{6,4},{7,5},{8,10},{9,11},{10,... | collective-permute-start | bytes 933896 | tf_op jit(solution)/shard_map/ppermute | solution.py:350
  41.9 5.7 %all-to-all-start.3 = ((bf16[8,104,256]{2,1,0:T(8,128)(2,1)}), bf16[8,104,256]{2,1,0:T(8,128)(2,1)S(1)}, u32[]{:S(2)}, u32[]{:S(2)}) async-start(bf16[8,104,256]{2,1,0:T(8,128)(2,1)} %shard_map.234), calls=%async_computation.3 | async-start | bytes 851968 | tf_op jit(solution)/shard_map/all_to_all | solution.py:373
  47.6 2.5 %collective-permute-done.10.refs_6_.refs_2_ = bf16[8,152,128]{2,1,0:T(8,128)(2,1)S(1)} collective-permute-done((bf16[8,152,128]{2,1,0:T(8,128)(2,1)S(1)}, bf16[8,152,128]{2,1,0:T(8,128)(2,1)S(1)}, u32[]{:S(2)}, u32[]{:S(2)}) %collective-permute-start.10) | collective-permute-done | bytes 311328 | tf_op jit(solution)/shard_map/ppermute | solution.py:350
  50.6 1.7 %collective-permute-done.7.refs_1_ = bf16[192,768]{1,0:T(8,128)(2,1)S(1)} collective-permute-done((bf16[192,768]{1,0:T(8,128)(2,1)}, bf16[192,768]{1,0:T(8,128)(2,1)S(1)}, u32[]{:S(2)}, u32[]{:S(2)}) %collective-permute-start.7) | collective-permute-done | bytes 294944 | tf_op jit(solution)/shard_map/ppermute | solution.py:350
  53.7 3.8 %shard_map.235 = (f32[768,192]{1,0:T(8,128)S(1)}, f32[8,128]{1,0:T(8,128)S(1)}, f32[8,128]{1,0:T(8,128)S(1)}) custom-call(s32[4]{0:T(128)S(1)} %copy-done.4, bf16[192,768]{1,0:T(8,128)(2,1)S(1)} %bitcast.8, bf16[192,768]{1,0:T(8,128)(2,1)S(1)} %collective-permute-done.7.refs_1_, bf16[192,768]{1,0:T(8,128)(2,1)} %collective-permute-done.refs_2_, ...), custom_call_target="tpu_custom_call" | custom-call | flops 1000000000 | bytes 1024 | tf_op jit(solution)/shard_map/pallas_call | solution.py:201
  58.3 1.1 %collective-permute-start.13 = (f32[8,128]{1,0:T(8,128)S(1)}, f32[8,128]{1,0:T(8,128)S(1)}, u32[]{:S(2)}, u32[]{:S(2)}) collective-permute-start(f32[8,128]{1,0:T(8,128)S(1)} %get-tuple-element.46.refs_0_), channel_id=1, source_target_pairs={{0,2},{1,3},{2,0},{3,1},{4,6},{5,7},{6,4},{7,5},{8,10},{9,11},{10,... | collective-permute-start | bytes 12296 | tf_op jit(solution)/shard_map/ppermute | solution.py:350
  59.5 3.1 %shard_map.236 = (f32[1,192,768]{2,1,0:T(8,128)}, f32[1,256,1024]{2,1,0:T(8,128)}) custom-call(s32[4]{0:T(128)S(1)} %copy-done.3, bf16[8,104,256]{2,1,0:T(8,128)(2,1)S(1)} %all-to-all-done.1.refs_4_.refs_0_, bf16[8,104,256]{2,1,0:T(8,128)(2,1)S(1)} %collective-permute-done.2.refs_5_.refs_1_, bf16[8,104,256]{2,1,0:T(8,128)(2,1)S(1)} %collective-permute-done.5.refs_6_.refs_2_, ...), custom_call_target="tpu_custom_call" | custom-call | flops 1073741824 | bytes 5373952 | tf_op jit(solution)/shard_map/pallas_call | solution.py:273
  63.5 5.7 %all-to-all-start.2 = ((bf16[8,144,128]{2,1,0:T(8,128)(2,1)}), bf16[8,144,128]{2,1,0:T(8,128)(2,1)S(1)}, u32[]{:S(2)}, u32[]{:S(2)}) async-start(bf16[8,144,128]{2,1,0:T(8,128)(2,1)} %shard_map.237), calls=%async_computation.2 | async-start | bytes 589824 | tf_op jit(solution)/shard_map/all_to_all | solution.py:373
  69.9 1.2 %collective-permute-start.17 = (f32[4,8,128]{2,1,0:T(8,128)S(1)}, f32[4,8,128]{2,1,0:T(8,128)S(1)}, u32[]{:S(2)}, u32[]{:S(2)}) collective-permute-start(f32[4,8,128]{2,1,0:T(8,128)S(1)} %get-tuple-element.51.refs_1_), channel_id=1, source_target_pairs={{0,3},{1,2},{2,1},{3,0},{4,7},{5,6},{6,5},{7,4},{8,11},{9,10},{10,... | collective-permute-start | bytes 49160 | tf_op jit(solution)/shard_map/ppermute | solution.py:350
  71.8 2.8 %shard_map.241 = f32[1,2,192,768]{3,2,1,0:T(8,128)} custom-call(s32[4]{0:T(128)S(1)} %copy-done.4, bf16[8,152,128]{2,1,0:T(8,128)(2,1)S(1)} %all-to-all-done.refs_4_.refs_0_, bf16[8,152,128]{2,1,0:T(8,128)(2,1)S(1)} %collective-permute-done.9.refs_5_.refs_1_, bf16[8,152,128]{2,1,0:T(8,128)(2,1)S(1)} %collective-permute-done.10.refs_6_.refs_2_, ...), custom_call_target="tpu_custom_call" | custom-call | flops 452984832 | bytes 3538944 | tf_op jit(solution)/shard_map/pallas_call | solution.py:273
  74.8 1.4 %shard_map.240 = f32[4,96,256]{2,1,0:T(8,128)} custom-call(s32[4]{0:T(128)S(1)} %copy-done.3, f32[4,96,256]{2,1,0:T(8,128)S(1)} %copy-done, bf16[8,104,256]{2,1,0:T(8,128)(2,1)S(1)} %all-to-all-done.3.back, f32[4,8,128]{2,1,0:T(8,128)S(1)} %get-tuple-element.50.refs_0_, f32[4,8,128]{2,1,0:T(8,128)S(1)} %get-tuple-element.51.refs_1_, ...), custom_call_target="tpu_custom_call" | custom-call | flops 196608 | bytes 1179648 | tf_op jit(solution)/shard_map/pallas_call | solution.py:309
  76.2 3.2 %all-to-all-done.2.back = bf16[8,144,128]{2,1,0:T(8,128)(2,1)S(1)} async-done(((bf16[8,144,128]{2,1,0:T(8,128)(2,1)}), bf16[8,144,128]{2,1,0:T(8,128)(2,1)S(1)}, u32[]{:S(2)}, u32[]{:S(2)}) %all-to-all-start.2) | async-done | bytes 294944 | tf_op jit(solution)/shard_map/all_to_all | solution.py:373
  79.4 1.4 %shard_map.238 = f32[4,96,192]{2,1,0:T(8,128)} custom-call(s32[4]{0:T(128)S(1)} %copy-done.4, f32[4,96,192]{2,1,0:T(8,128)S(1)} %copy-done.1, bf16[8,144,128]{2,1,0:T(8,128)(2,1)S(1)} %all-to-all-done.2.back), custom_call_target="tpu_custom_call" | custom-call | flops 147456 | bytes 884736 | tf_op jit(solution)/shard_map/pallas_call | solution.py:309
  (48 shorter events, 7.5 us)
Async XLA Ops:
  0.6 12.1 %collective-permute-start = (bf16[192,768]{1,0:T(8,128)(2,1)}, bf16[192,768]{1,0:T(8,128)(2,1)}, u32[]{:S(2)}, u32[]{:S(2)}) collective-permute-start(bf16[192,768]{1,0:T(8,128)(2,1)} %bitcast.6), channel_id=1, source_target_pairs={{0,2},{1,3},{2,0},{3,1},{4,6},{5,7},{6,4},{7,5},{8,10},{9,11},{10,... | collective-permute-start | bytes 884744 | tf_op jit(solution)/shard_map/ppermute | solution.py:350
  3.7 13.5 %collective-permute-start.1 = (bf16[192,768]{1,0:T(8,128)(2,1)}, bf16[192,768]{1,0:T(8,128)(2,1)S(1)}, u32[]{:S(2)}, u32[]{:S(2)}) collective-permute-start(bf16[192,768]{1,0:T(8,128)(2,1)} %bitcast.3), channel_id=1, source_target_pairs={{0,2},{1,3},{2,0},{3,1},{4,6},{5,7},{6,4},{7,5},{8,10},{9,11},{10,... | collective-permute-start | bytes 884744 | tf_op jit(solution)/shard_map/ppermute | solution.py:350
  6.5 18.2 %all-to-all-start.1 = ((bf16[8,104,256]{2,1,0:T(8,128)(2,1)}), bf16[8,104,256]{2,1,0:T(8,128)(2,1)S(1)}, u32[]{:S(2)}, u32[]{:S(2)}) async-start(bf16[8,104,256]{2,1,0:T(8,128)(2,1)} %get-tuple-element.34), calls=%async_computation.1 | async-start | bytes 851968 | tf_op jit(solution)/shard_map/all_to_all | solution.py:373
  12.7 20.3 %copy-start.2 = (bf16[1,192,768]{2,1,0:T(8,128)(2,1)S(1)}, bf16[1,192,768]{2,1,0:T(8,128)(2,1)}, u32[]{:S(2)}) copy-start(bf16[1,192,768]{2,1,0:T(8,128)(2,1)} %param.30) | copy-start | bytes 884740
  12.7 22.9 %copy-start.3 = (s32[4]{0:T(128)S(1)}, s32[4]{0:T(128)}, u32[]{:S(2)}) copy-start(s32[4]{0:T(128)} %owner.16) | copy-start | bytes 52
  24.7 8.3 %collective-permute-start.5 = (bf16[8,104,256]{2,1,0:T(8,128)(2,1)S(1)}, bf16[8,104,256]{2,1,0:T(8,128)(2,1)S(1)}, u32[]{:S(2)}, u32[]{:S(2)}) collective-permute-start(bf16[8,104,256]{2,1,0:T(8,128)(2,1)S(1)} %all-to-all-done.1.refs_4_.refs_0_), channel_id=1, source_target_pairs={{0,2},{1,3},{2,0},{3,1},{4,6},{5,7},{6,4},{7,5},{8,10},{9,11},{10,... | collective-permute-start | bytes 1277960 | tf_op jit(solution)/shard_map/ppermute | solution.py:350
  26.1 6.9 %collective-permute-start.2 = (bf16[8,104,256]{2,1,0:T(8,128)(2,1)S(1)}, bf16[8,104,256]{2,1,0:T(8,128)(2,1)S(1)}, u32[]{:S(2)}, u32[]{:S(2)}) collective-permute-start(bf16[8,104,256]{2,1,0:T(8,128)(2,1)S(1)} %all-to-all-done.1.refs_4_.refs_0_), channel_id=1, source_target_pairs={{0,1},{1,0},{2,3},{3,2},{4,5},{5,4},{6,7},{7,6},{8,9},{9,8},{10,11... | collective-permute-start | bytes 1277960 | tf_op jit(solution)/shard_map/ppermute | solution.py:350
  26.1 14.2 %all-to-all-start = ((bf16[8,152,128]{2,1,0:T(8,128)(2,1)}), bf16[8,152,128]{2,1,0:T(8,128)(2,1)S(1)}, u32[]{:S(2)}, u32[]{:S(2)}) async-start(bf16[8,152,128]{2,1,0:T(8,128)(2,1)} %get-tuple-element.33), calls=%async_computation | async-start | bytes 622592 | tf_op jit(solution)/shard_map/all_to_all | solution.py:373
  33.0 2.6 %collective-permute-start.6 = (bf16[8,104,256]{2,1,0:T(8,128)(2,1)S(1)}, bf16[8,104,256]{2,1,0:T(8,128)(2,1)S(1)}, u32[]{:S(2)}, u32[]{:S(2)}) collective-permute-start(bf16[8,104,256]{2,1,0:T(8,128)(2,1)S(1)} %collective-permute-done.5.refs_6_.refs_2_), channel_id=1, source_target_pairs={{0,1},{1,0},{2,3},{3,2},{4,5},{5,4},{6,7},{7,6},{8,9},{9,8},{10,11... | collective-permute-start | bytes 1277960 | tf_op jit(solution)/shard_map/ppermute | solution.py:350
  33.0 2.2 %collective-permute-start.3 = (bf16[192,768]{1,0:T(8,128)(2,1)S(1)}, bf16[192,768]{1,0:T(8,128)(2,1)S(1)}, u32[]{:S(2)}, u32[]{:S(2)}) collective-permute-start(bf16[192,768]{1,0:T(8,128)(2,1)S(1)} %bitcast.4), channel_id=1, source_target_pairs={{0,1},{1,0},{2,3},{3,2},{4,5},{5,4},{6,7},{7,6},{8,9},{9,8},{10,11... | collective-permute-start | bytes 884744 | tf_op jit(solution)/shard_map/ppermute | solution.py:350
  33.5 2.1 %collective-permute-start.4 = (bf16[192,768]{1,0:T(8,128)(2,1)S(1)}, bf16[192,768]{1,0:T(8,128)(2,1)S(1)}, u32[]{:S(2)}, u32[]{:S(2)}) collective-permute-start(bf16[192,768]{1,0:T(8,128)(2,1)S(1)} %collective-permute-done.1.refs_2_), channel_id=1, source_target_pairs={{0,1},{1,0},{2,3},{3,2},{4,5},{5,4},{6,7},{7,6},{8,9},{9,8},{10,11... | collective-permute-start | bytes 884744 | tf_op jit(solution)/shard_map/ppermute | solution.py:350
  40.3 1.6 %collective-permute-start.9 = (bf16[8,152,128]{2,1,0:T(8,128)(2,1)S(1)}, bf16[8,152,128]{2,1,0:T(8,128)(2,1)S(1)}, u32[]{:S(2)}, u32[]{:S(2)}) collective-permute-start(bf16[8,152,128]{2,1,0:T(8,128)(2,1)S(1)} %all-to-all-done.refs_4_.refs_0_), channel_id=1, source_target_pairs={{0,1},{1,0},{2,3},{3,2},{4,5},{5,4},{6,7},{7,6},{8,9},{9,8},{10,11... | collective-permute-start | bytes 933896 | tf_op jit(solution)/shard_map/ppermute | solution.py:350
  40.3 9.8 %collective-permute-start.10 = (bf16[8,152,128]{2,1,0:T(8,128)(2,1)S(1)}, bf16[8,152,128]{2,1,0:T(8,128)(2,1)S(1)}, u32[]{:S(2)}, u32[]{:S(2)}) collective-permute-start(bf16[8,152,128]{2,1,0:T(8,128)(2,1)S(1)} %all-to-all-done.refs_4_.refs_0_), channel_id=1, source_target_pairs={{0,2},{1,3},{2,0},{3,1},{4,6},{5,7},{6,4},{7,5},{8,10},{9,11},{10,... | collective-permute-start | bytes 933896 | tf_op jit(solution)/shard_map/ppermute | solution.py:350
  41.9 21.6 %all-to-all-start.3 = ((bf16[8,104,256]{2,1,0:T(8,128)(2,1)}), bf16[8,104,256]{2,1,0:T(8,128)(2,1)S(1)}, u32[]{:S(2)}, u32[]{:S(2)}) async-start(bf16[8,104,256]{2,1,0:T(8,128)(2,1)} %shard_map.234), calls=%async_computation.3 | async-start | bytes 851968 | tf_op jit(solution)/shard_map/all_to_all | solution.py:373
  50.1 2.7 %collective-permute-start.11 = (bf16[8,152,128]{2,1,0:T(8,128)(2,1)S(1)}, bf16[8,152,128]{2,1,0:T(8,128)(2,1)S(1)}, u32[]{:S(2)}, u32[]{:S(2)}) collective-permute-start(bf16[8,152,128]{2,1,0:T(8,128)(2,1)S(1)} %collective-permute-done.10.refs_6_.refs_2_), channel_id=1, source_target_pairs={{0,1},{1,0},{2,3},{3,2},{4,5},{5,4},{6,7},{7,6},{8,9},{9,8},{10,11... | collective-permute-start | bytes 933896 | tf_op jit(solution)/shard_map/ppermute | solution.py:350
  50.1 2.2 %collective-permute-start.7 = (bf16[192,768]{1,0:T(8,128)(2,1)}, bf16[192,768]{1,0:T(8,128)(2,1)S(1)}, u32[]{:S(2)}, u32[]{:S(2)}) collective-permute-start(bf16[192,768]{1,0:T(8,128)(2,1)} %bitcast.7), channel_id=1, source_target_pairs={{0,1},{1,0},{2,3},{3,2},{4,5},{5,4},{6,7},{7,6},{8,9},{9,8},{10,11... | collective-permute-start | bytes 884744 | tf_op jit(solution)/shard_map/ppermute | solution.py:350
  50.6 2.1 %collective-permute-start.8 = (bf16[192,768]{1,0:T(8,128)(2,1)}, bf16[192,768]{1,0:T(8,128)(2,1)S(1)}, u32[]{:S(2)}, u32[]{:S(2)}) collective-permute-start(bf16[192,768]{1,0:T(8,128)(2,1)} %collective-permute-done.refs_2_), channel_id=1, source_target_pairs={{0,1},{1,0},{2,3},{3,2},{4,5},{5,4},{6,7},{7,6},{8,9},{9,8},{10,11... | collective-permute-start | bytes 884744 | tf_op jit(solution)/shard_map/ppermute | solution.py:350
  57.5 5.1 %collective-permute-start.14 = (f32[8,128]{1,0:T(8,128)S(1)}, f32[8,128]{1,0:T(8,128)S(1)}, u32[]{:S(2)}, u32[]{:S(2)}) collective-permute-start(f32[8,128]{1,0:T(8,128)S(1)} %get-tuple-element.46.refs_0_), channel_id=1, source_target_pairs={{0,3},{1,2},{2,1},{3,0},{4,7},{5,6},{6,5},{7,4},{8,11},{9,10},{10,... | collective-permute-start | bytes 12296 | tf_op jit(solution)/shard_map/ppermute | solution.py:350
  58.3 4.3 %collective-permute-start.13 = (f32[8,128]{1,0:T(8,128)S(1)}, f32[8,128]{1,0:T(8,128)S(1)}, u32[]{:S(2)}, u32[]{:S(2)}) collective-permute-start(f32[8,128]{1,0:T(8,128)S(1)} %get-tuple-element.46.refs_0_), channel_id=1, source_target_pairs={{0,2},{1,3},{2,0},{3,1},{4,6},{5,7},{6,4},{7,5},{8,10},{9,11},{10,... | collective-permute-start | bytes 12296 | tf_op jit(solution)/shard_map/ppermute | solution.py:350
  59.4 3.2 %collective-permute-start.12 = (f32[8,128]{1,0:T(8,128)S(1)}, f32[8,128]{1,0:T(8,128)S(1)}, u32[]{:S(2)}, u32[]{:S(2)}) collective-permute-start(f32[8,128]{1,0:T(8,128)S(1)} %get-tuple-element.46.refs_0_), channel_id=1, source_target_pairs={{0,1},{1,0},{2,3},{3,2},{4,5},{5,4},{6,7},{7,6},{8,9},{9,8},{10,11... | collective-permute-start | bytes 12296 | tf_op jit(solution)/shard_map/ppermute | solution.py:350
  63.5 15.9 %all-to-all-start.2 = ((bf16[8,144,128]{2,1,0:T(8,128)(2,1)}), bf16[8,144,128]{2,1,0:T(8,128)(2,1)S(1)}, u32[]{:S(2)}, u32[]{:S(2)}) async-start(bf16[8,144,128]{2,1,0:T(8,128)(2,1)} %shard_map.237), calls=%async_computation.2 | async-start | bytes 589824 | tf_op jit(solution)/shard_map/all_to_all | solution.py:373
  69.9 4.8 %collective-permute-start.17 = (f32[4,8,128]{2,1,0:T(8,128)S(1)}, f32[4,8,128]{2,1,0:T(8,128)S(1)}, u32[]{:S(2)}, u32[]{:S(2)}) collective-permute-start(f32[4,8,128]{2,1,0:T(8,128)S(1)} %get-tuple-element.51.refs_1_), channel_id=1, source_target_pairs={{0,3},{1,2},{2,1},{3,0},{4,7},{5,6},{6,5},{7,4},{8,11},{9,10},{10,... | collective-permute-start | bytes 49160 | tf_op jit(solution)/shard_map/ppermute | solution.py:350
  71.1 3.7 %collective-permute-start.16 = (f32[4,8,128]{2,1,0:T(8,128)S(1)}, f32[4,8,128]{2,1,0:T(8,128)S(1)}, u32[]{:S(2)}, u32[]{:S(2)}) collective-permute-start(f32[4,8,128]{2,1,0:T(8,128)S(1)} %get-tuple-element.51.refs_1_), channel_id=1, source_target_pairs={{0,2},{1,3},{2,0},{3,1},{4,6},{5,7},{6,4},{7,5},{8,10},{9,11},{10,... | collective-permute-start | bytes 49160 | tf_op jit(solution)/shard_map/ppermute | solution.py:350
  71.8 3.1 %collective-permute-start.15 = (f32[4,8,128]{2,1,0:T(8,128)S(1)}, f32[4,8,128]{2,1,0:T(8,128)S(1)}, u32[]{:S(2)}, u32[]{:S(2)}) collective-permute-start(f32[4,8,128]{2,1,0:T(8,128)S(1)} %get-tuple-element.51.refs_1_), channel_id=1, source_target_pairs={{0,1},{1,0},{2,3},{3,2},{4,5},{5,4},{6,7},{7,6},{8,9},{9,8},{10,11... | collective-permute-start | bytes 49160 | tf_op jit(solution)/shard_map/ppermute | solution.py:350
  (7 other events, 64.8 us)
where the time goes:
time: 81.5 us; the launch traced here: 80.8 us
  starting transfers between devices  31.8 us (39%)
  waiting for transfers between devices  24.6 us (30%)
  Pallas kernels  22.6 us (28%)
  local copies, waits for them, and re-layouts  1 us (1%)
    all_to_all x4, starting transfers between devices, over_shard(): lax.all_to_all(value, 'shard', split_axis=0, concat_axis=0, tiled=True)  21.2 us
    ppermute x18, waiting for transfers between devices, flip(): return lax.ppermute(value, 'tensor', [(i, i ^ bits) for i in range(size)])  15.1 us
    ppermute x18, starting transfers between devices, flip(): return lax.ppermute(value, 'tensor', [(i, i ^ bits) for i in range(size)])  10.6 us
    all_to_all x4, waiting for transfers between devices, over_shard(): lax.all_to_all(value, 'shard', split_axis=0, concat_axis=0, tiled=True)  9.5 us
    pallas_call x2, Pallas kernels, shampoo_part(): pl.pallas_call(functools.partial(shampoo_kernel, rows, cols, turned, embe...  7.86 us
    pallas_call x2, Pallas kernels, stats_part(): pl.pallas_call(functools.partial(stats_kernel, rows, cols, len(stats) ==...  5.93 us
    pallas_call x2, Pallas kernels, adam_part(): pl.pallas_call(adam_kernel, out_shape=(jax.ShapeDtypeStruct((owners, *pac...  4.5 us
    pallas_call x2, Pallas kernels, weight_part(): pl.pallas_call(weight_kernel, out_shape=jax.ShapeDtypeStruct(weight.shape...  2.79 us
  transfers between devices with their start and end apart: 22, of which 12 were waited for; matrix products, arithmetic and copies ran while one was open for 0% of the time, Pallas kernels for 26%

commit v1 on v0

--- a/solution.py
+++ b/solution.py
@@ -146,14 +146,12 @@
 def shampoo_kernel(rows, cols, turned, embed, owner, *refs):
     tensor = lax.axis_size("tensor")
     left, grad = refs[:tensor], refs[tensor : 2 * tensor]
-    root_hbm, *outs, whole, blocks, done, root, arrived = refs[2 * tensor :]
+    root, *outs, whole, blocks, done = refs[2 * tensor :]
     part = lax.axis_index("tensor")
 
     @pl.when(holds(owner))
     def _():
         depth = left[0].shape[0]
-        fetch = pltpu.make_async_copy(root_hbm, root, arrived)
-        fetch.start()
         adam_sq = jnp.zeros((1, 1), f32)
         for k in range(tensor):
             band = pl.ds(pl.multiple_of((part ^ k) * depth, depth), depth)
@@ -161,7 +159,6 @@
             blocks[part ^ k] = unpack(grad[k], rows, cols)
             adam_sq = adam_sq + unpack_total(grad[k], rows, cols, 0)
         half = jnp.zeros((whole.shape[0], cols), f32)
-        fetch.wait()
         for k in range(tensor):
             span = slice(k * cols, (k + 1) * cols)
             if turned:
@@ -201,18 +198,18 @@
     return pl.pallas_call(
         functools.partial(shampoo_kernel, rows, cols, turned, embed),
         out_shape=shapes,
-        in_specs=[SMEM] + [VMEM] * (2 * tensor) + [HBM],
+        in_specs=[SMEM] + [VMEM] * (2 * tensor + 1),
         out_specs=(VMEM,) * len(shapes),
         scratch_shapes=[
             pltpu.VMEM((depth, depth), bf16),
             pltpu.VMEM((tensor, depth, cols), bf16),
             pltpu.VMEM((depth, cols) if embed else (8, LANES), f32),
-            pltpu.VMEM(root.shape, bf16),
-            pltpu.SemaphoreType.DMA(()),
         ],
         compiler_params=LIMIT,
-        cost_estimate=BRIEF,
-    )(owner, *left, *grad, in_hbm(root))
+        cost_estimate=pl.CostEstimate(
+            flops=1_000_000_000 if embed else 2_000_000_000, bytes_accessed=1024, transcendentals=0
+        ),
+    )(owner, *left, *grad, root)
 
 
 def stats_kernel(rows, cols, paired, owner, *refs):
@@ -280,8 +277,8 @@
         + [pltpu.SemaphoreType.DMA((2,)), pltpu.SemaphoreType.DMA((2,))],
         compiler_params=LIMIT,
         cost_estimate=pl.CostEstimate(
-            flops=4 * depth * depth * cols,
-            bytes_accessed=8 * sum(value.size for value in stats) + 2 * depth * depth,
+            flops=1_000_000_000,
+            bytes_accessed=1024,
             transcendentals=0,
         ),
     )(owner, *grad, *[in_hbm(value) for value in stats])
@@ -441,17 +438,17 @@
     (glu_done,) = shampoo_part(glu_owner, glu_left, glu_grad, glu_right_root, rows, True)
     att_near, att_far = spread_first(after(over_shard(att_packed), glu_done))
     att_left = spread_rest(*lax.optimization_barrier((att_root, att_root_far, att_near))[:2])
-    att_grad = spread_rest(att_near, att_far)
-    glu_back = over_shard(after(glu_done, att_grad[1]))
-    att_done = shampoo_part(att_owner, att_left, att_grad, att_right_root, rows, False)
+    att_beside = flip(att_near, 1)
+    glu_back = over_shard(after(glu_done, att_beside))
     glu_left_out, glu_right_out = stats_part(
         glu_owner,
-        [after(glu_grad[0], att_done[0]), *glu_grad[1:]],
+        [after(glu_grad[0], att_beside), *glu_grad[1:]],
         (glu_left_stat, glu_right_stat),
         rows,
         glu_weight.shape[2],
     )
-    att_done = (after(att_done[0], glu_left_out), *att_done[1:])
+    att_grad = spread_rest(att_near, after(att_far, glu_left_out, *att_left[1:]))
+    att_done = shampoo_part(att_owner, att_left, att_grad, att_right_root, rows, False)
     (att_stats_out,) = stats_part(att_owner, att_grad, (att_stats,), rows, att_weight.shape[2])
     att_back = over_shard(grafted(*att_done, owners))
     glu_totals = totals_part(glu_owner, glu_back, rows, glu_weight.shape[2])

time: 81.5 us -> 75.1 us (0.921)
  starting transfers between devices: 31.8 us -> 27.6 us
  Pallas kernels: 22.6 us -> 21.3 us
  local copies, waits for them, and re-layouts: 1 us -> 0.05 us
    all_to_all x4, starting transfers between devices: 21.2 us -> 17.4 us  [over_shard(): lax.all_to_all(value, 'shard', split_axis=0, concat_axis=0, tiled=True)]
    pallas_call x2, Pallas kernels: 7.86 us -> 6.08 us  [shampoo_part(): pl.pallas_call(functools.partial(shampoo_kernel, rows, cols, turned, embe...]
    unnamed x18 -> x22, local copies, waits for them, and re-layouts: 1 us -> 0.05 us
  transfers between devices with their start and end apart: 22 -> 22, of which waited for: 12 -> 12; matrix products, arithmetic and copies ran while one was open for 0% -> 0% of each run, Pallas kernels for 26% -> 27%
where the time goes in v1:
time: 75.1 us; the launch traced here: 74.5 us
  starting transfers between devices  27.6 us (37%)
  waiting for transfers between devices  24.8 us (33%)
  Pallas kernels  21.3 us (28%)
  between operations  0.83 us (1%)
    all_to_all x4, starting transfers between devices, over_shard(): lax.all_to_all(value, 'shard', split_axis=0, concat_axis=0, tiled=True)  17.4 us
    ppermute x18, waiting for transfers between devices, flip(): return lax.ppermute(value, 'tensor', [(i, i ^ bits) for i in range(size)])  15.7 us
    ppermute x18, starting transfers between devices, flip(): return lax.ppermute(value, 'tensor', [(i, i ^ bits) for i in range(size)])  10.1 us
    all_to_all x4, waiting for transfers between devices, over_shard(): lax.all_to_all(value, 'shard', split_axis=0, concat_axis=0, tiled=True)  9.1 us
    pallas_call x2, Pallas kernels, stats_part(): pl.pallas_call(functools.partial(stats_kernel, rows, cols, len(stats) ==...  6.37 us
    pallas_call x2, Pallas kernels, shampoo_part(): pl.pallas_call(functools.partial(shampoo_kernel, rows, cols, turned, embe...  6.08 us
    pallas_call x2, Pallas kernels, adam_part(): pl.pallas_call(adam_kernel, out_shape=(jax.ShapeDtypeStruct((owners, *pac...  4.49 us
    pallas_call x2, Pallas kernels, weight_part(): pl.pallas_call(weight_kernel, out_shape=jax.ShapeDtypeStruct(weight.shape...  2.79 us
  transfers between devices with their start and end apart: 22, of which 12 were waited for; matrix products, arithmetic and copies ran while one was open for 0% of the time, Pallas kernels for 27%

profile of v1, /device:TPU:0, one launch (start us, length us, event | category | flops | bytes accessed | tf_op | source)
XLA Modules:
  0.0 74.5 jit_solution(12876908889176427957)
XLA Ops:
  0.6 3.0 %collective-permute-start = (bf16[192,768]{1,0:T(8,128)(2,1)}, bf16[192,768]{1,0:T(8,128)(2,1)}, u32[]{:S(2)}, u32[]{:S(2)}) collective-permute-start(bf16[192,768]{1,0:T(8,128)(2,1)} %bitcast.6), channel_id=1, source_target_pairs={{0,2},{1,3},{2,0},{3,1},{4,6},{5,7},{6,4},{7,5},{8,10},{9,11},{10,... | collective-permute-start | bytes 884744 | tf_op jit(solution)/shard_map/ppermute | solution.py:347
  3.8 2.7 %shard_map.233 = (bf16[8,104,256]{2,1,0:T(8,128)(2,1)}, f32[4,96,256]{2,1,0:T(8,128)}, f32[4,96,256]{2,1,0:T(8,128)}) custom-call(s32[4]{0:T(128)} %owner.16, f32[2,4,96,256]{3,2,1,0:T(8,128)} %grads.2, f32[4,96,256]{2,1,0:T(8,128)} %moment.3, f32[4,96,256]{2,1,0:T(8,128)} %second.3), custom_call_target="tpu_custom_call" | custom-call | flops 10000000000 | bytes 3145728 | tf_op jit(solution)/shard_map/pallas_call | solution.py:122
  6.5 6.2 %all-to-all-start.1 = ((bf16[8,104,256]{2,1,0:T(8,128)(2,1)}), bf16[8,104,256]{2,1,0:T(8,128)(2,1)S(1)}, u32[]{:S(2)}, u32[]{:S(2)}) async-start(bf16[8,104,256]{2,1,0:T(8,128)(2,1)} %get-tuple-element.34), calls=%async_computation.1 | async-start | bytes 851968 | tf_op jit(solution)/shard_map/all_to_all | solution.py:370
  12.7 4.5 %collective-permute-done.1.refs_2_ = bf16[192,768]{1,0:T(8,128)(2,1)S(1)} collective-permute-done((bf16[192,768]{1,0:T(8,128)(2,1)}, bf16[192,768]{1,0:T(8,128)(2,1)S(1)}, u32[]{:S(2)}, u32[]{:S(2)}) %collective-permute-start.1) | collective-permute-done | bytes 294944 | tf_op jit(solution)/shard_map/ppermute | solution.py:347
  17.2 1.8 %shard_map.232 = (bf16[8,152,128]{2,1,0:T(8,128)(2,1)}, f32[4,96,192]{2,1,0:T(8,128)}, f32[4,96,192]{2,1,0:T(8,128)}) custom-call(s32[4]{0:T(128)S(1)} %copy-done.5, f32[2,4,96,192]{3,2,1,0:T(8,128)S(1)} %copy-done.6, f32[4,96,192]{2,1,0:T(8,128)S(1)} %copy-done.7, f32[4,96,192]{2,1,0:T(8,128)S(1)} %copy-done.8), custom_call_target="tpu_custom_call" | custom-call | flops 10000000000 | bytes 2359296 | tf_op jit(solution)/shard_map/pallas_call | solution.py:122
  19.0 5.7 %all-to-all-done.1.refs_4_.refs_0_ = bf16[8,104,256]{2,1,0:T(8,128)(2,1)S(1)} async-done(((bf16[8,104,256]{2,1,0:T(8,128)(2,1)}), bf16[8,104,256]{2,1,0:T(8,128)(2,1)S(1)}, u32[]{:S(2)}, u32[]{:S(2)}) %all-to-all-start.1) | async-done | bytes 426016 | tf_op jit(solution)/shard_map/all_to_all | solution.py:370
  24.7 1.4 %collective-permute-start.5 = (bf16[8,104,256]{2,1,0:T(8,128)(2,1)S(1)}, bf16[8,104,256]{2,1,0:T(8,128)(2,1)S(1)}, u32[]{:S(2)}, u32[]{:S(2)}) collective-permute-start(bf16[8,104,256]{2,1,0:T(8,128)(2,1)S(1)} %all-to-all-done.1.refs_4_.refs_0_), channel_id=1, source_target_pairs={{0,2},{1,3},{2,0},{3,1},{4,6},{5,7},{6,4},{7,5},{8,10},{9,11},{10,... | collective-permute-start | bytes 1277960 | tf_op jit(solution)/shard_map/ppermute | solution.py:347
  26.1 3.6 %all-to-all-start = ((bf16[8,152,128]{2,1,0:T(8,128)(2,1)}), bf16[8,152,128]{2,1,0:T(8,128)(2,1)S(1)}, u32[]{:S(2)}, u32[]{:S(2)}) async-start(bf16[8,152,128]{2,1,0:T(8,128)(2,1)} %get-tuple-element.33), calls=%async_computation | async-start | bytes 622592 | tf_op jit(solution)/shard_map/all_to_all | solution.py:370
  29.7 3.3 %collective-permute-done.5.refs_6_.refs_2_ = bf16[8,104,256]{2,1,0:T(8,128)(2,1)S(1)} collective-permute-done((bf16[8,104,256]{2,1,0:T(8,128)(2,1)S(1)}, bf16[8,104,256]{2,1,0:T(8,128)(2,1)S(1)}, u32[]{:S(2)}, u32[]{:S(2)}) %collective-permute-start.5) | collective-permute-done | bytes 426016 | tf_op jit(solution)/shard_map/ppermute | solution.py:347
  33.6 1.6 %collective-permute-done.3.refs_1_ = bf16[192,768]{1,0:T(8,128)(2,1)S(1)} collective-permute-done((bf16[192,768]{1,0:T(8,128)(2,1)S(1)}, bf16[192,768]{1,0:T(8,128)(2,1)S(1)}, u32[]{:S(2)}, u32[]{:S(2)}) %collective-permute-start.3) | collective-permute-done | bytes 294944 | tf_op jit(solution)/shard_map/ppermute | solution.py:347
  35.6 3.0 %shard_map.234 = bf16[8,104,256]{2,1,0:T(8,128)(2,1)} custom-call(s32[4]{0:T(128)S(1)} %copy-done.4, bf16[192,768]{1,0:T(8,128)(2,1)S(1)} %bitcast.5, bf16[192,768]{1,0:T(8,128)(2,1)S(1)} %collective-permute-done.3.refs_1_, bf16[192,768]{1,0:T(8,128)(2,1)S(1)} %collective-permute-done.1.refs_2_, bf16[192,768]{1,0:T(8,128)(2,1)S(1)} %collective-permute-done.4.refs_3_, ...), custom_call_target="tpu_custom_call" | custom-call | flops 1000000000 | bytes 1024 | tf_op jit(solution)/shard_map/pallas_call | solution.py:198
  38.6 1.7 %all-to-all-done.refs_4_.refs_0_ = bf16[8,152,128]{2,1,0:T(8,128)(2,1)S(1)} async-done(((bf16[8,152,128]{2,1,0:T(8,128)(2,1)}), bf16[8,152,128]{2,1,0:T(8,128)(2,1)S(1)}, u32[]{:S(2)}, u32[]{:S(2)}) %all-to-all-start) | async-done | bytes 311328 | tf_op jit(solution)/shard_map/all_to_all | solution.py:370
  41.9 3.6 %all-to-all-start.3 = ((bf16[8,104,256]{2,1,0:T(8,128)(2,1)}), bf16[8,104,256]{2,1,0:T(8,128)(2,1)S(1)}, u32[]{:S(2)}, u32[]{:S(2)}) async-start(bf16[8,104,256]{2,1,0:T(8,128)(2,1)} %shard_map.234), calls=%async_computation.3 | async-start | bytes 851968 | tf_op jit(solution)/shard_map/all_to_all | solution.py:370
  45.6 3.1 %shard_map.235 = (f32[1,192,768]{2,1,0:T(8,128)}, f32[1,256,1024]{2,1,0:T(8,128)}) custom-call(s32[4]{0:T(128)S(1)} %copy-done.4, bf16[8,104,256]{2,1,0:T(8,128)(2,1)S(1)} %all-to-all-done.1.refs_4_.refs_0_, bf16[8,104,256]{2,1,0:T(8,128)(2,1)S(1)} %collective-permute-done.2.refs_5_.refs_1_, bf16[8,104,256]{2,1,0:T(8,128)(2,1)S(1)} %collective-permute-done.5.refs_6_.refs_2_, ...), custom_call_target="tpu_custom_call" | custom-call | flops 1000000000 | bytes 1024 | tf_op jit(solution)/shard_map/pallas_call | solution.py:270
  48.7 1.5 %collective-permute-done.10.refs_6_.refs_2_ = bf16[8,152,128]{2,1,0:T(8,128)(2,1)} collective-permute-done((bf16[8,152,128]{2,1,0:T(8,128)(2,1)S(1)}, bf16[8,152,128]{2,1,0:T(8,128)(2,1)}, u32[]{:S(2)}, u32[]{:S(2)}) %collective-permute-start.10) | collective-permute-done | bytes 311328 | tf_op jit(solution)/shard_map/ppermute | solution.py:347
  50.2 1.8 %collective-permute-done.11.refs_7_.refs_3_ = bf16[8,152,128]{2,1,0:T(8,128)(2,1)S(1)} collective-permute-done((bf16[8,152,128]{2,1,0:T(8,128)(2,1)}, bf16[8,152,128]{2,1,0:T(8,128)(2,1)S(1)}, u32[]{:S(2)}, u32[]{:S(2)}) %collective-permute-start.11) | collective-permute-done | bytes 311328 | tf_op jit(solution)/shard_map/ppermute | solution.py:347
  52.0 3.1 %shard_map.236 = (f32[768,192]{1,0:T(8,128)S(1)}, f32[8,128]{1,0:T(8,128)S(1)}, f32[8,128]{1,0:T(8,128)S(1)}) custom-call(s32[4]{0:T(128)S(1)} %copy-done.5, bf16[192,768]{1,0:T(8,128)(2,1)S(1)} %bitcast.8, bf16[192,768]{1,0:T(8,128)(2,1)} %collective-permute-done.7.refs_1_, bf16[192,768]{1,0:T(8,128)(2,1)} %collective-permute-done.refs_2_, ...), custom_call_target="tpu_custom_call" | custom-call | flops 2000000000 | bytes 1024 | tf_op jit(solution)/shard_map/pallas_call | solution.py:198
  55.6 1.4 %collective-permute-start.13 = (f32[8,128]{1,0:T(8,128)S(1)}, f32[8,128]{1,0:T(8,128)S(1)}, u32[]{:S(2)}, u32[]{:S(2)}) collective-permute-start(f32[8,128]{1,0:T(8,128)S(1)} %get-tuple-element.46.refs_0_), channel_id=1, source_target_pairs={{0,2},{1,3},{2,0},{3,1},{4,6},{5,7},{6,4},{7,5},{8,10},{9,11},{10,... | collective-permute-start | bytes 12296 | tf_op jit(solution)/shard_map/ppermute | solution.py:347
  57.0 1.2 %collective-permute-done.14.refs_3_ = f32[8,128]{1,0:T(8,128)S(1)} collective-permute-done((f32[8,128]{1,0:T(8,128)S(1)}, f32[8,128]{1,0:T(8,128)S(1)}, u32[]{:S(2)}, u32[]{:S(2)}) %collective-permute-start.14) | collective-permute-done | bytes 4128 | tf_op jit(solution)/shard_map/ppermute | solution.py:347
  60.1 4.0 %all-to-all-start.2 = ((bf16[8,144,128]{2,1,0:T(8,128)(2,1)}), bf16[8,144,128]{2,1,0:T(8,128)(2,1)S(1)}, u32[]{:S(2)}, u32[]{:S(2)}) async-start(bf16[8,144,128]{2,1,0:T(8,128)(2,1)} %shard_map.237), calls=%async_computation.2 | async-start | bytes 589824 | tf_op jit(solution)/shard_map/all_to_all | solution.py:370
  66.7 3.2 %shard_map.241 = f32[1,2,192,768]{3,2,1,0:T(8,128)} custom-call(s32[4]{0:T(128)S(1)} %copy-done.5, bf16[8,152,128]{2,1,0:T(8,128)(2,1)S(1)} %all-to-all-done.refs_4_.refs_0_, bf16[8,152,128]{2,1,0:T(8,128)(2,1)S(1)} %collective-permute-done.9.refs_5_.refs_1_, bf16[8,152,128]{2,1,0:T(8,128)(2,1)} %collective-permute-done.10.refs_6_.refs_2_, ...), custom_call_target="tpu_custom_call" | custom-call | flops 1000000000 | bytes 1024 | tf_op jit(solution)/shard_map/pallas_call | solution.py:270
  70.0 1.4 %shard_map.240 = f32[4,96,256]{2,1,0:T(8,128)} custom-call(s32[4]{0:T(128)S(1)} %copy-done.4, f32[4,96,256]{2,1,0:T(8,128)S(1)} %copy-done.1, bf16[8,104,256]{2,1,0:T(8,128)(2,1)S(1)} %all-to-all-done.3.back, f32[4,8,128]{2,1,0:T(8,128)S(1)} %get-tuple-element.50.refs_0_, f32[4,8,128]{2,1,0:T(8,128)S(1)} %get-tuple-element.51.refs_1_, ...), custom_call_target="tpu_custom_call" | custom-call | flops 196608 | bytes 1179648 | tf_op jit(solution)/shard_map/pallas_call | solution.py:306
  71.4 1.7 %all-to-all-done.2.back = bf16[8,144,128]{2,1,0:T(8,128)(2,1)S(1)} async-done(((bf16[8,144,128]{2,1,0:T(8,128)(2,1)}), bf16[8,144,128]{2,1,0:T(8,128)(2,1)S(1)}, u32[]{:S(2)}, u32[]{:S(2)}) %all-to-all-start.2) | async-done | bytes 294944 | tf_op jit(solution)/shard_map/all_to_all | solution.py:370
  73.1 1.4 %shard_map.238 = f32[4,96,192]{2,1,0:T(8,128)} custom-call(s32[4]{0:T(128)S(1)} %copy-done.5, f32[4,96,192]{2,1,0:T(8,128)S(1)} %copy-done.2, bf16[8,144,128]{2,1,0:T(8,128)(2,1)S(1)} %all-to-all-done.2.back), custom_call_target="tpu_custom_call" | custom-call | flops 147456 | bytes 884736 | tf_op jit(solution)/shard_map/pallas_call | solution.py:306
  (52 shorter events, 7.8 us)
Async XLA Ops:
  0.6 12.1 %collective-permute-start = (bf16[192,768]{1,0:T(8,128)(2,1)}, bf16[192,768]{1,0:T(8,128)(2,1)}, u32[]{:S(2)}, u32[]{:S(2)}) collective-permute-start(bf16[192,768]{1,0:T(8,128)(2,1)} %bitcast.6), channel_id=1, source_target_pairs={{0,2},{1,3},{2,0},{3,1},{4,6},{5,7},{6,4},{7,5},{8,10},{9,11},{10,... | collective-permute-start | bytes 884744 | tf_op jit(solution)/shard_map/ppermute | solution.py:347
  3.7 13.5 %collective-permute-start.1 = (bf16[192,768]{1,0:T(8,128)(2,1)}, bf16[192,768]{1,0:T(8,128)(2,1)S(1)}, u32[]{:S(2)}, u32[]{:S(2)}) collective-permute-start(bf16[192,768]{1,0:T(8,128)(2,1)} %bitcast.3), channel_id=1, source_target_pairs={{0,2},{1,3},{2,0},{3,1},{4,6},{5,7},{6,4},{7,5},{8,10},{9,11},{10,... | collective-permute-start | bytes 884744 | tf_op jit(solution)/shard_map/ppermute | solution.py:347
  6.5 18.2 %all-to-all-start.1 = ((bf16[8,104,256]{2,1,0:T(8,128)(2,1)}), bf16[8,104,256]{2,1,0:T(8,128)(2,1)S(1)}, u32[]{:S(2)}, u32[]{:S(2)}) async-start(bf16[8,104,256]{2,1,0:T(8,128)(2,1)} %get-tuple-element.34), calls=%async_computation.1 | async-start | bytes 851968 | tf_op jit(solution)/shard_map/all_to_all | solution.py:370
  12.7 22.9 %copy-start = (bf16[1,1024,256]{2,1,0:T(8,128)(2,1)S(1)}, bf16[1,1024,256]{2,1,0:T(8,128)(2,1)}, u32[]{:S(2)}) copy-start(bf16[1,1024,256]{2,1,0:T(8,128)(2,1)} %refs_8_.1) | copy-start | bytes 1572868
  12.7 22.9 %copy-start.4 = (s32[4]{0:T(128)S(1)}, s32[4]{0:T(128)}, u32[]{:S(2)}) copy-start(s32[4]{0:T(128)} %owner.16) | copy-start | bytes 52
  24.7 8.3 %collective-permute-start.5 = (bf16[8,104,256]{2,1,0:T(8,128)(2,1)S(1)}, bf16[8,104,256]{2,1,0:T(8,128)(2,1)S(1)}, u32[]{:S(2)}, u32[]{:S(2)}) collective-permute-start(bf16[8,104,256]{2,1,0:T(8,128)(2,1)S(1)} %all-to-all-done.1.refs_4_.refs_0_), channel_id=1, source_target_pairs={{0,2},{1,3},{2,0},{3,1},{4,6},{5,7},{6,4},{7,5},{8,10},{9,11},{10,... | collective-permute-start | bytes 1277960 | tf_op jit(solution)/shard_map/ppermute | solution.py:347
  26.1 6.9 %collective-permute-start.2 = (bf16[8,104,256]{2,1,0:T(8,128)(2,1)S(1)}, bf16[8,104,256]{2,1,0:T(8,128)(2,1)S(1)}, u32[]{:S(2)}, u32[]{:S(2)}) collective-permute-start(bf16[8,104,256]{2,1,0:T(8,128)(2,1)S(1)} %all-to-all-done.1.refs_4_.refs_0_), channel_id=1, source_target_pairs={{0,1},{1,0},{2,3},{3,2},{4,5},{5,4},{6,7},{7,6},{8,9},{9,8},{10,11... | collective-permute-start | bytes 1277960 | tf_op jit(solution)/shard_map/ppermute | solution.py:347
  26.1 14.2 %all-to-all-start = ((bf16[8,152,128]{2,1,0:T(8,128)(2,1)}), bf16[8,152,128]{2,1,0:T(8,128)(2,1)S(1)}, u32[]{:S(2)}, u32[]{:S(2)}) async-start(bf16[8,152,128]{2,1,0:T(8,128)(2,1)} %get-tuple-element.33), calls=%async_computation | async-start | bytes 622592 | tf_op jit(solution)/shard_map/all_to_all | solution.py:370
  33.0 2.6 %collective-permute-start.6 = (bf16[8,104,256]{2,1,0:T(8,128)(2,1)S(1)}, bf16[8,104,256]{2,1,0:T(8,128)(2,1)S(1)}, u32[]{:S(2)}, u32[]{:S(2)}) collective-permute-start(bf16[8,104,256]{2,1,0:T(8,128)(2,1)S(1)} %collective-permute-done.5.refs_6_.refs_2_), channel_id=1, source_target_pairs={{0,1},{1,0},{2,3},{3,2},{4,5},{5,4},{6,7},{7,6},{8,9},{9,8},{10,11... | collective-permute-start | bytes 1277960 | tf_op jit(solution)/shard_map/ppermute | solution.py:347
  33.0 2.2 %collective-permute-start.3 = (bf16[192,768]{1,0:T(8,128)(2,1)S(1)}, bf16[192,768]{1,0:T(8,128)(2,1)S(1)}, u32[]{:S(2)}, u32[]{:S(2)}) collective-permute-start(bf16[192,768]{1,0:T(8,128)(2,1)S(1)} %bitcast.4), channel_id=1, source_target_pairs={{0,1},{1,0},{2,3},{3,2},{4,5},{5,4},{6,7},{7,6},{8,9},{9,8},{10,11... | collective-permute-start | bytes 884744 | tf_op jit(solution)/shard_map/ppermute | solution.py:347
  33.5 2.1 %collective-permute-start.4 = (bf16[192,768]{1,0:T(8,128)(2,1)S(1)}, bf16[192,768]{1,0:T(8,128)(2,1)S(1)}, u32[]{:S(2)}, u32[]{:S(2)}) collective-permute-start(bf16[192,768]{1,0:T(8,128)(2,1)S(1)} %collective-permute-done.1.refs_2_), channel_id=1, source_target_pairs={{0,1},{1,0},{2,3},{3,2},{4,5},{5,4},{6,7},{7,6},{8,9},{9,8},{10,11... | collective-permute-start | bytes 884744 | tf_op jit(solution)/shard_map/ppermute | solution.py:347
  40.3 1.6 %collective-permute-start.9 = (bf16[8,152,128]{2,1,0:T(8,128)(2,1)S(1)}, bf16[8,152,128]{2,1,0:T(8,128)(2,1)S(1)}, u32[]{:S(2)}, u32[]{:S(2)}) collective-permute-start(bf16[8,152,128]{2,1,0:T(8,128)(2,1)S(1)} %all-to-all-done.refs_4_.refs_0_), channel_id=1, source_target_pairs={{0,1},{1,0},{2,3},{3,2},{4,5},{5,4},{6,7},{7,6},{8,9},{9,8},{10,11... | collective-permute-start | bytes 933896 | tf_op jit(solution)/shard_map/ppermute | solution.py:347
  40.3 9.9 %collective-permute-start.10 = (bf16[8,152,128]{2,1,0:T(8,128)(2,1)S(1)}, bf16[8,152,128]{2,1,0:T(8,128)(2,1)}, u32[]{:S(2)}, u32[]{:S(2)}) collective-permute-start(bf16[8,152,128]{2,1,0:T(8,128)(2,1)S(1)} %all-to-all-done.refs_4_.refs_0_), channel_id=1, source_target_pairs={{0,2},{1,3},{2,0},{3,1},{4,6},{5,7},{6,4},{7,5},{8,10},{9,11},{10,... | collective-permute-start | bytes 933896 | tf_op jit(solution)/shard_map/ppermute | solution.py:347
  41.0 7.7 %collective-permute-start.7 = (bf16[192,768]{1,0:T(8,128)(2,1)}, bf16[192,768]{1,0:T(8,128)(2,1)}, u32[]{:S(2)}, u32[]{:S(2)}) collective-permute-start(bf16[192,768]{1,0:T(8,128)(2,1)} %bitcast.7), channel_id=1, source_target_pairs={{0,1},{1,0},{2,3},{3,2},{4,5},{5,4},{6,7},{7,6},{8,9},{9,8},{10,11... | collective-permute-start | bytes 884744 | tf_op jit(solution)/shard_map/ppermute | solution.py:347
  41.2 7.5 %collective-permute-start.8 = (bf16[192,768]{1,0:T(8,128)(2,1)}, bf16[192,768]{1,0:T(8,128)(2,1)}, u32[]{:S(2)}, u32[]{:S(2)}) collective-permute-start(bf16[192,768]{1,0:T(8,128)(2,1)} %collective-permute-done.refs_2_), channel_id=1, source_target_pairs={{0,1},{1,0},{2,3},{3,2},{4,5},{5,4},{6,7},{7,6},{8,9},{9,8},{10,11... | collective-permute-start | bytes 884744 | tf_op jit(solution)/shard_map/ppermute | solution.py:347
  41.9 18.2 %all-to-all-start.3 = ((bf16[8,104,256]{2,1,0:T(8,128)(2,1)}), bf16[8,104,256]{2,1,0:T(8,128)(2,1)S(1)}, u32[]{:S(2)}, u32[]{:S(2)}) async-start(bf16[8,104,256]{2,1,0:T(8,128)(2,1)} %shard_map.234), calls=%async_computation.3 | async-start | bytes 851968 | tf_op jit(solution)/shard_map/all_to_all | solution.py:370
  50.2 1.8 %collective-permute-start.11 = (bf16[8,152,128]{2,1,0:T(8,128)(2,1)}, bf16[8,152,128]{2,1,0:T(8,128)(2,1)S(1)}, u32[]{:S(2)}, u32[]{:S(2)}) collective-permute-start(bf16[8,152,128]{2,1,0:T(8,128)(2,1)} %collective-permute-done.10.refs_6_.refs_2_), channel_id=1, source_target_pairs={{0,1},{1,0},{2,3},{3,2},{4,5},{5,4},{6,7},{7,6},{8,9},{9,8},{10,11... | collective-permute-start | bytes 933896 | tf_op jit(solution)/shard_map/ppermute | solution.py:347
  55.1 3.1 %collective-permute-start.14 = (f32[8,128]{1,0:T(8,128)S(1)}, f32[8,128]{1,0:T(8,128)S(1)}, u32[]{:S(2)}, u32[]{:S(2)}) collective-permute-start(f32[8,128]{1,0:T(8,128)S(1)} %get-tuple-element.46.refs_0_), channel_id=1, source_target_pairs={{0,3},{1,2},{2,1},{3,0},{4,7},{5,6},{6,5},{7,4},{8,11},{9,10},{10,... | collective-permute-start | bytes 12296 | tf_op jit(solution)/shard_map/ppermute | solution.py:347
  55.6 3.6 %collective-permute-start.13 = (f32[8,128]{1,0:T(8,128)S(1)}, f32[8,128]{1,0:T(8,128)S(1)}, u32[]{:S(2)}, u32[]{:S(2)}) collective-permute-start(f32[8,128]{1,0:T(8,128)S(1)} %get-tuple-element.46.refs_0_), channel_id=1, source_target_pairs={{0,2},{1,3},{2,0},{3,1},{4,6},{5,7},{6,4},{7,5},{8,10},{9,11},{10,... | collective-permute-start | bytes 12296 | tf_op jit(solution)/shard_map/ppermute | solution.py:347
  57.0 2.2 %collective-permute-start.12 = (f32[8,128]{1,0:T(8,128)S(1)}, f32[8,128]{1,0:T(8,128)S(1)}, u32[]{:S(2)}, u32[]{:S(2)}) collective-permute-start(f32[8,128]{1,0:T(8,128)S(1)} %get-tuple-element.46.refs_0_), channel_id=1, source_target_pairs={{0,1},{1,0},{2,3},{3,2},{4,5},{5,4},{6,7},{7,6},{8,9},{9,8},{10,11... | collective-permute-start | bytes 12296 | tf_op jit(solution)/shard_map/ppermute | solution.py:347
  60.1 13.0 %all-to-all-start.2 = ((bf16[8,144,128]{2,1,0:T(8,128)(2,1)}), bf16[8,144,128]{2,1,0:T(8,128)(2,1)S(1)}, u32[]{:S(2)}, u32[]{:S(2)}) async-start(bf16[8,144,128]{2,1,0:T(8,128)(2,1)} %shard_map.237), calls=%async_computation.2 | async-start | bytes 589824 | tf_op jit(solution)/shard_map/all_to_all | solution.py:370
  64.8 5.2 %collective-permute-start.17 = (f32[4,8,128]{2,1,0:T(8,128)S(1)}, f32[4,8,128]{2,1,0:T(8,128)S(1)}, u32[]{:S(2)}, u32[]{:S(2)}) collective-permute-start(f32[4,8,128]{2,1,0:T(8,128)S(1)} %get-tuple-element.51.refs_1_), channel_id=1, source_target_pairs={{0,3},{1,2},{2,1},{3,0},{4,7},{5,6},{6,5},{7,4},{8,11},{9,10},{10,... | collective-permute-start | bytes 49160 | tf_op jit(solution)/shard_map/ppermute | solution.py:347
  64.9 5.1 %collective-permute-start.16 = (f32[4,8,128]{2,1,0:T(8,128)S(1)}, f32[4,8,128]{2,1,0:T(8,128)S(1)}, u32[]{:S(2)}, u32[]{:S(2)}) collective-permute-start(f32[4,8,128]{2,1,0:T(8,128)S(1)} %get-tuple-element.51.refs_1_), channel_id=1, source_target_pairs={{0,2},{1,3},{2,0},{3,1},{4,6},{5,7},{6,4},{7,5},{8,10},{9,11},{10,... | collective-permute-start | bytes 49160 | tf_op jit(solution)/shard_map/ppermute | solution.py:347
  66.0 4.0 %collective-permute-start.15 = (f32[4,8,128]{2,1,0:T(8,128)S(1)}, f32[4,8,128]{2,1,0:T(8,128)S(1)}, u32[]{:S(2)}, u32[]{:S(2)}) collective-permute-start(f32[4,8,128]{2,1,0:T(8,128)S(1)} %get-tuple-element.51.refs_1_), channel_id=1, source_target_pairs={{0,1},{1,0},{2,3},{3,2},{4,5},{5,4},{6,7},{7,6},{8,9},{9,8},{10,11... | collective-permute-start | bytes 49160 | tf_op jit(solution)/shard_map/ppermute | solution.py:347
  (9 other events, 95.8 us)
